TPU v7x, 32 devices: a whole 2x2x4 slice. The times are simulated.
32 devices in a mesh: rows: 4 (over y, x), cols: 8 (over z, core).
Axes of the slice: x: 2, y: 2, z: 4, core: 2. Of those that a mesh axis runs over, the one named last changes fastest.
Arguments:
- heat_excess: float32 [8, 1024, 4096], P(None, ('rows', 'cols')), may hold values from -6 to 6
- square_region_label: int32 [1024, 4096], P(('rows', 'cols')), may hold values from 0 to 63
- region_heating_flux: float32 [64], replicated, may hold values from 0.05 to 0.5
- layer_substance_label: int32 [8], replicated, may hold values from 0 to 3, as said below
- sideways_coupling_factor: float32 [4], replicated, may hold values from 0.08 to 0.2
- upward_coupling_factor: float32 [4], replicated, may hold values from 0.02 to 0.08
- layer_heating_fraction: float32 [4], replicated, may hold values from 0.1 to 0.6
Outputs:
- ending_heat_excess: float32 [8, 1024, 4096], P(None, 'rows', 'cols')
Inputs may be any that keep to these rules, and one draw needn't show every extreme that they name: `layer_substance_label`: each material is named by exactly 2 tiers.
All inputs are finite; a program needn't handle non-finite values.
Results may differ from a plain program's by a relative error of at most 0.00002.
Values sent between devices are 32-bit elements; how exact they have to be, the bound alone decides.
A program may use at most 192 MiB of HBM per device.

v0:
```python
import jax
import jax.numpy as jnp
from jax import lax
from jax.experimental import pallas as pl
from jax.experimental.pallas import tpu as pltpu
from jax.sharding import PartitionSpec as P

EPOCH_TOTAL = 8
HALO = 8
LANES = 128


def kernel(
    rows,
    cols,
    heat,
    label,
    flux_tab,
    tier_lab,
    lat_tab,
    vert_tab,
    share_tab,
    out,
    ext,
    lab_ext,
    dens,
    buf,
    mask,
    res,
    in_sem,
    halo_send,
    halo_recv,
    send_sem,
    recv_sem,
    own_sem,
):
    tiers, height, breadth = heat.shape
    tall = height + 2 * HALO
    width = breadth // cols
    wide = width + 2 * LANES
    r = lax.axis_index("rows")
    c = lax.axis_index("cols")
    me = r * cols + c
    total = rows * cols
    has_prev = me > 0
    has_next = me < total - 1
    prev = lax.rem(me + total - 1, total)
    nxt = lax.rem(me + 1, total)
    prev_id = (prev // cols, lax.rem(prev, cols))
    next_id = (nxt // cols, lax.rem(nxt, cols))
    MESH = pl.DeviceIdType.MESH

    own_heat = pltpu.make_async_copy(
        heat, ext.at[:, pl.ds(HALO, height), pl.ds(LANES, breadth)], in_sem.at[0]
    )
    own_heat.start()
    own_lab = pltpu.make_async_copy(
        label, lab_ext.at[pl.ds(HALO, height), pl.ds(LANES, breadth)], in_sem.at[1]
    )
    own_lab.start()

    barrier = pltpu.get_barrier_semaphore()
    for j in range(1, cols):
        pl.semaphore_signal(
            barrier, inc=1, device_id=(r, lax.rem(c + j, cols)), device_id_type=MESH
        )
    far_prev = has_prev & (c == 0)
    far_next = has_next & (c == cols - 1)

    @pl.when(far_prev)
    def _():
        pl.semaphore_signal(barrier, inc=1, device_id=prev_id, device_id_type=MESH)

    @pl.when(far_next)
    def _():
        pl.semaphore_signal(barrier, inc=1, device_id=next_id, device_id_type=MESH)

    pl.semaphore_wait(
        barrier, cols - 1 + far_prev.astype(jnp.int32) + far_next.astype(jnp.int32)
    )

    inner = pl.ds(LANES, breadth)
    top, bottom = pl.ds(0, HALO), pl.ds(HALO + height, HALO)

    def halo(src_rows, dst_rows, where, slot):
        return (
            pltpu.make_async_remote_copy(
                src_ref=heat.at[:, src_rows, :],
                dst_ref=ext.at[:, dst_rows, inner],
                send_sem=halo_send.at[2 * slot],
                recv_sem=halo_recv.at[2 * slot],
                device_id=where,
                device_id_type=MESH,
            ),
            pltpu.make_async_remote_copy(
                src_ref=label.at[src_rows, :],
                dst_ref=lab_ext.at[dst_rows, inner],
                send_sem=halo_send.at[2 * slot + 1],
                recv_sem=halo_recv.at[2 * slot + 1],
                device_id=where,
                device_id_type=MESH,
            ),
        )

    down = halo(pl.ds(height - HALO, HALO), top, next_id, 0)
    up = halo(pl.ds(0, HALO), bottom, prev_id, 1)

    @pl.when(has_next)
    def _():
        for copy in down:
            copy.start()

    @pl.when(has_prev)
    def _():
        for copy in up:
            copy.start()

    @pl.when(jnp.logical_not(has_prev))
    def _():
        ext[:, 0:HALO, :] = jnp.zeros((tiers, HALO, breadth + 2 * LANES), jnp.float32)
        lab_ext[0:HALO, :] = jnp.zeros((HALO, breadth + 2 * LANES), jnp.int32)

    @pl.when(jnp.logical_not(has_next))
    def _():
        ext[:, HALO + height :, :] = jnp.zeros(
            (tiers, HALO, breadth + 2 * LANES), jnp.float32
        )
        lab_ext[HALO + height :, :] = jnp.zeros(
            (HALO, breadth + 2 * LANES), jnp.int32
        )

    for at in (0, LANES + breadth):
        ext[:, HALO : HALO + height, at : at + LANES] = jnp.zeros(
            (tiers, height, LANES), jnp.float32
        )
        dens[:, at : at + LANES] = jnp.zeros((tall, LANES), jnp.float32)

    @pl.when(has_prev)
    def _():
        for at in (0, LANES + breadth):
            ext[:, 0:HALO, at : at + LANES] = jnp.zeros(
                (tiers, HALO, LANES), jnp.float32
            )

    @pl.when(has_next)
    def _():
        for at in (0, LANES + breadth):
            ext[:, HALO + height :, at : at + LANES] = jnp.zeros(
                (tiers, HALO, LANES), jnp.float32
            )

    blocks = flux_tab.shape[0]
    piece = 4 * LANES

    def look_up(first, count):
        def one(i, carry):
            at = pl.ds(pl.multiple_of(LANES + i * piece, LANES), piece)
            ids = lab_ext[first : first + count, at]
            found = jnp.zeros((count, piece), jnp.float32)
            for b in range(blocks):
                found = jnp.where(ids == b, flux_tab[b], found)
            dens[first : first + count, at] = found
            return carry

        lax.fori_loop(0, breadth // piece, one, 0)

    own_lab.wait()
    for first in range(HALO, HALO + height, HALO):
        look_up(first, HALO)

    @pl.when(has_prev)
    def _():
        for copy in down:
            copy.wait_recv()

    @pl.when(has_next)
    def _():
        for copy in up:
            copy.wait_recv()

    look_up(0, HALO)
    look_up(HALO + height, HALO)
    own_heat.wait()

    lat = [lat_tab[tier_lab[k]] for k in range(tiers)]
    vert = [vert_tab[tier_lab[k]] for k in range(tiers)]
    share = [share_tab[tier_lab[k]] for k in range(tiers)]

    def send(dest):
        return pltpu.make_async_remote_copy(
            src_ref=res.at[dest],
            dst_ref=out.at[:, pl.ds(pl.multiple_of(c * height, HALO), height), :],
            send_sem=send_sem.at[dest],
            recv_sem=recv_sem.at[c],
            device_id=(r, dest),
            device_id_type=MESH,
        )

    def compute(dest):
        base = pl.multiple_of(dest * width, LANES)
        window = pl.ds(base, wide)
        row_pos = me * height - HALO + lax.broadcasted_iota(jnp.int32, (tall, wide), 0)
        col_pos = base - LANES + lax.broadcasted_iota(jnp.int32, (tall, wide), 1)
        ok = (row_pos >= 0) & (row_pos < total * height)
        ok = ok & (col_pos >= 0) & (col_pos < breadth)
        mask[...] = jnp.where(ok, 1.0, 0.0)

        def step(read, store):
            for g in range(tall // HALO):
                lo = g * HALO
                here = slice(lo, lo + HALO)
                before = slice(max(lo - HALO, 0), max(lo - HALO, 0) + HALO)
                last = min(lo + HALO, tall - HALO)
                after = slice(last, last + HALO)
                power = dens[here, window]
                inside = mask[here, :]
                edge = lax.broadcasted_iota(jnp.int32, (HALO, wide), 0)
                centre = read(0, here)
                flux_below = None
                for k in range(tiers):
                    above = read(k + 1, here) if k + 1 < tiers else None
                    north = jnp.where(
                        edge == 0,
                        pltpu.roll(read(k, before), 1, 0),
                        pltpu.roll(centre, 1, 0),
                    )
                    south = jnp.where(
                        edge == HALO - 1,
                        pltpu.roll(read(k, after), HALO - 1, 0),
                        pltpu.roll(centre, HALO - 1, 0),
                    )
                    beside = north + south
                    beside = beside + pltpu.roll(centre, 1, 1)
                    beside = beside + pltpu.roll(centre, wide - 1, 1)
                    rise = -centre if above is None else above - centre
                    flux = vert[k] * rise
                    fresh = centre * (1.0 - 4.0 * lat[k]) + lat[k] * beside
                    fresh = fresh + flux
                    if flux_below is not None:
                        fresh = fresh - flux_below
                    fresh = fresh + share[k] * power
                    store(k, here, fresh * inside)
                    flux_below = flux
                    centre = above

        def from_buf(which):
            return lambda k, at: buf[which, k, at, :]

        def to_buf(which):
            def put(k, at, value):
                buf[which, k, at, :] = value

            return put

        def load(k, carry):
            buf[0, k] = ext[k, :, window]
            return carry

        lax.fori_loop(0, tiers, load, 0)

        def pair(i, carry):
            step(from_buf(0), to_buf(1))
            step(from_buf(1), to_buf(0))
            return carry

        lax.fori_loop(0, EPOCH_TOTAL // 2, pair, 0)

        def keep(k, carry):
            res[dest, k] = buf[0, k, HALO : HALO + height, LANES : LANES + width]
            return carry

        lax.fori_loop(0, tiers, keep, 0)

    half = max(cols // 2, 1)
    side = c // half

    def dest_of(i):
        far = lax.rem(side + 1, 2) * half + lax.rem(c + i, half)
        j = i - half
        quarter = half // 2
        late = jnp.where(j < half - 1, j - (half - quarter) + 1, 0)
        off = jnp.where(j < half - quarter, j + quarter, late)
        near = side * half + lax.rem(c + off, half)
        return jnp.where(i < half, far, near)

    def one_chunk(i, carry):
        dest = dest_of(i)
        compute(dest)
        send(dest).start()
        return carry

    lax.fori_loop(0, cols - 1, one_chunk, 0)
    compute(c)
    own = pltpu.make_async_copy(
        res.at[c],
        out.at[:, pl.ds(pl.multiple_of(c * height, HALO), height), :],
        own_sem.at[0],
    )
    own.start()

    @pl.when(has_next)
    def _():
        for copy in down:
            copy.wait_send()

    @pl.when(has_prev)
    def _():
        for copy in up:
            copy.wait_send()

    def finish(j, carry):
        other = lax.rem(c + j, cols)
        pltpu.make_async_remote_copy(
            src_ref=res.at[other],
            dst_ref=out.at[:, pl.ds(pl.multiple_of(other * height, HALO), height), :],
            send_sem=send_sem.at[other],
            recv_sem=recv_sem.at[other],
            device_id=(r, other),
            device_id_type=MESH,
        ).wait()
        return carry

    lax.fori_loop(1, cols, finish, 0)
    own.wait()


def solution(mesh):
    rows, cols = mesh.shape["rows"], mesh.shape["cols"]

    def body(heat, label, flux_tab, tier_lab, lat_tab, vert_tab, share_tab):
        tiers, height, breadth = heat.shape
        tall = height + 2 * HALO
        width = breadth // cols
        wide = width + 2 * LANES
        smem = pl.BlockSpec(memory_space=pltpu.SMEM)
        hbm = pl.BlockSpec(memory_space=pl.ANY)
        dma = pltpu.SemaphoreType.DMA

        def run(*refs):
            kernel(rows, cols, *refs)

        return pl.pallas_call(
            run,
            out_shape=jax.ShapeDtypeStruct((tiers, height * cols, width), jnp.float32),
            in_specs=[hbm, hbm, smem, smem, smem, smem, smem],
            out_specs=hbm,
            scratch_shapes=[
                pltpu.VMEM((tiers, tall, breadth + 2 * LANES), jnp.float32),
                pltpu.VMEM((tall, breadth + 2 * LANES), jnp.int32),
                pltpu.VMEM((tall, breadth + 2 * LANES), jnp.float32),
                pltpu.VMEM((2, tiers, tall, wide), jnp.float32),
                pltpu.VMEM((tall, wide), jnp.float32),
                pltpu.VMEM((cols, tiers, height, width), jnp.float32),
                dma((2,)),
                dma((4,)),
                dma((4,)),
                dma((cols,)),
                dma((cols,)),
                dma((1,)),
            ],
            compiler_params=pltpu.CompilerParams(
                collective_id=0, has_side_effects=True, vmem_limit_bytes=48 * 2**20
            ),
        )(heat, label, flux_tab, tier_lab, lat_tab, vert_tab, share_tab)

    return jax.shard_map(
        body,
        mesh=mesh,
        in_specs=(
            P(None, ("rows", "cols"), None),
            P(("rows", "cols"), None),
            P(),
            P(),
            P(),
            P(),
            P(),
        ),
        out_specs=P(None, "rows", "cols"),
        check_vma=False,
    )
```

profile of v0, /device:TPU:19, one launch (start us, length us, event | category | flops | bytes accessed | tf_op | source)
XLA Modules:
  0.0 136.7 jit_solution(10802031116949667309)
XLA Ops:
  0.0 0.0 copy-start
  0.0 1.0 copy-done
  1.0 0.0 copy-start.1
  1.0 0.7 copy-done.1
  1.7 0.0 copy-start.2
  1.7 0.7 copy-done.2
  2.4 0.0 copy-start.3
  2.4 0.7 copy-done.3
  3.0 0.0 copy-start.4
  3.0 0.7 copy-done.4
  3.7 0.0 copy-start.5
  3.7 0.7 copy-done.5
  4.3 130.4 %shard_map.73 = f32[8,256,512]{2,1,0:T(8,128)S(1)} custom-call(f32[8,32,4096]{2,1,0:T(8,128)} %refs_0_.1, s32[32,4096]{1,0:T(8,128)S(1)} %copy-done, f32[64]{0:T(128)S(1)} %copy-done.1, s32[8]{0:T(128)S(1)} %copy-done.2, f32[4]{0:T(128)S(1)} %copy-done.3, f32[4]{0:T(128)S(1)} %copy-done.4, f32[4]{0:T(128)S(1)} %copy-done.5), custom_call_target="tpu_custom_call" | custom-call | tf_op jit(solution)/shard_map/pallas_call | solution.py:342
  134.7 2.0 %copy.9 = f32[8,256,512]{2,1,0:T(8,128)} copy(f32[8,256,512]{2,1,0:T(8,128)S(1)} %shard_map.73) | data formatting | bytes 8388608
Async XLA Ops:
  0.0 1.0 copy-start
  1.0 0.7 copy-start.1
  1.7 0.7 copy-start.2
  2.4 0.7 copy-start.3
  3.0 0.7 copy-start.4
  3.7 0.7 copy-start.5
where the time goes:
time: 137 us
  Pallas kernels  130 us (95%)
  local copies, waits for them, and re-layouts  6.33 us (5%)
    pallas_call x1, Pallas kernels, body(): pl.pallas_call(run, out_shape=jax.ShapeDtypeStruct((tiers, height * cols,...  130 us
    unnamed x13, local copies, waits for them, and re-layouts  6.33 us

commit v1 on v0

--- a/solution.py
+++ b/solution.py
@@ -79,22 +79,37 @@
         barrier, cols - 1 + far_prev.astype(jnp.int32) + far_next.astype(jnp.int32)
     )
 
-    inner = pl.ds(LANES, breadth)
-    top, bottom = pl.ds(0, HALO), pl.ds(HALO + height, HALO)
-
-    def halo(src_rows, dst_rows, where, slot):
+    top, bottom = (0, HALO), (HALO + height, HALO)
+    half = max(cols // 2, 1)
+    middle = half * width
+    side = c // half
+
+    def spans(device):
+        low_first = device // half
+        first = (1 - low_first) * (middle - LANES)
+        rest = low_first * (middle + LANES)
+        return (first, middle + LANES), (rest, breadth - middle - LANES)
+
+    def halo(src_row, dst_rows, where, slot, span):
+        start, size = span
+        start = pl.multiple_of(start, LANES)
+        src = (pl.ds(src_row, HALO), pl.ds(start, size))
+        dst = (
+            pl.ds(dst_rows[0], dst_rows[1]),
+            pl.ds(pl.multiple_of(start + LANES, LANES), size),
+        )
         return (
             pltpu.make_async_remote_copy(
-                src_ref=heat.at[:, src_rows, :],
-                dst_ref=ext.at[:, dst_rows, inner],
+                src_ref=heat.at[:, src[0], src[1]],
+                dst_ref=ext.at[:, dst[0], dst[1]],
                 send_sem=halo_send.at[2 * slot],
                 recv_sem=halo_recv.at[2 * slot],
                 device_id=where,
                 device_id_type=MESH,
             ),
             pltpu.make_async_remote_copy(
-                src_ref=label.at[src_rows, :],
-                dst_ref=lab_ext.at[dst_rows, inner],
+                src_ref=label.at[src[0], src[1]],
+                dst_ref=lab_ext.at[dst[0], dst[1]],
                 send_sem=halo_send.at[2 * slot + 1],
                 recv_sem=halo_recv.at[2 * slot + 1],
                 device_id=where,
@@ -102,18 +117,23 @@
             ),
         )
 
-    down = halo(pl.ds(height - HALO, HALO), top, next_id, 0)
-    up = halo(pl.ds(0, HALO), bottom, prev_id, 1)
-
-    @pl.when(has_next)
-    def _():
-        for copy in down:
-            copy.start()
-
-    @pl.when(has_prev)
-    def _():
-        for copy in up:
-            copy.start()
+    def down(i, device):
+        return halo(height - HALO, top, next_id, i, spans(device)[i])
+
+    def up(i, device):
+        return halo(0, bottom, prev_id, 2 + i, spans(device)[i])
+
+    for i in range(2):
+
+        @pl.when(has_next)
+        def _():
+            for copy in reversed(down(i, next_id[1])):
+                copy.start()
+
+        @pl.when(has_prev)
+        def _():
+            for copy in reversed(up(i, prev_id[1])):
+                copy.start()
 
     @pl.when(jnp.logical_not(has_prev))
     def _():
@@ -152,35 +172,43 @@
     blocks = flux_tab.shape[0]
     piece = 4 * LANES
 
-    def look_up(first, count):
-        def one(i, carry):
-            at = pl.ds(pl.multiple_of(LANES + i * piece, LANES), piece)
-            ids = lab_ext[first : first + count, at]
-            found = jnp.zeros((count, piece), jnp.float32)
-            for b in range(blocks):
-                found = jnp.where(ids == b, flux_tab[b], found)
-            dens[first : first + count, at] = found
+    def look_up(at, first, count):
+        ids = lab_ext[first : first + count, at]
+        found = jnp.zeros(ids.shape, jnp.float32)
+        for b in range(blocks):
+            found = jnp.where(ids == b, flux_tab[b], found)
+        dens[first : first + count, at] = found
+
+    def own_density(i, carry):
+        at = pl.ds(pl.multiple_of(LANES + i * piece, LANES), piece)
+        for first in range(HALO, HALO + height, HALO):
+            look_up(at, first, HALO)
+        return carry
+
+    own_lab.wait()
+    lax.fori_loop(0, breadth // piece, own_density, 0)
+    own_heat.wait()
+
+    def take_halo(i):
+        @pl.when(has_prev)
+        def _():
+            for copy in down(i, c):
+                copy.wait_recv()
+
+        @pl.when(has_next)
+        def _():
+            for copy in up(i, c):
+                copy.wait_recv()
+
+        start, size = spans(c)[i]
+
+        def one(j, carry):
+            at = pl.ds(pl.multiple_of(LANES + start + j * LANES, LANES), LANES)
+            look_up(at, 0, HALO)
+            look_up(at, HALO + height, HALO)
             return carry
 
-        lax.fori_loop(0, breadth // piece, one, 0)
-
-    own_lab.wait()
-    for first in range(HALO, HALO + height, HALO):
-        look_up(first, HALO)
-
-    @pl.when(has_prev)
-    def _():
-        for copy in down:
-            copy.wait_recv()
-
-    @pl.when(has_next)
-    def _():
-        for copy in up:
-            copy.wait_recv()
-
-    look_up(0, HALO)
-    look_up(HALO + height, HALO)
-    own_heat.wait()
+        lax.fori_loop(0, size // LANES, one, 0)
 
     lat = [lat_tab[tier_lab[k]] for k in range(tiers)]
     vert = [vert_tab[tier_lab[k]] for k in range(tiers)]
@@ -271,9 +299,6 @@
 
         lax.fori_loop(0, tiers, keep, 0)
 
-    half = max(cols // 2, 1)
-    side = c // half
-
     def dest_of(i):
         far = lax.rem(side + 1, 2) * half + lax.rem(c + i, half)
         j = i - half
@@ -289,7 +314,10 @@
         send(dest).start()
         return carry
 
-    lax.fori_loop(0, cols - 1, one_chunk, 0)
+    take_halo(0)
+    lax.fori_loop(0, half, one_chunk, 0)
+    take_halo(1)
+    lax.fori_loop(half, cols - 1, one_chunk, 0)
     compute(c)
     own = pltpu.make_async_copy(
         res.at[c],
@@ -298,15 +326,17 @@
     )
     own.start()
 
-    @pl.when(has_next)
-    def _():
-        for copy in down:
-            copy.wait_send()
-
-    @pl.when(has_prev)
-    def _():
-        for copy in up:
-            copy.wait_send()
+    for i in range(2):
+
+        @pl.when(has_next)
+        def _():
+            for copy in down(i, next_id[1]):
+                copy.wait_send()
+
+        @pl.when(has_prev)
+        def _():
+            for copy in up(i, prev_id[1]):
+                copy.wait_send()
 
     def finish(j, carry):
         other = lax.rem(c + j, cols)
@@ -352,8 +382,8 @@
                 pltpu.VMEM((tall, wide), jnp.float32),
                 pltpu.VMEM((cols, tiers, height, width), jnp.float32),
                 dma((2,)),
-                dma((4,)),
-                dma((4,)),
+                dma((8,)),
+                dma((8,)),
                 dma((cols,)),
                 dma((cols,)),
                 dma((1,)),

time: 137 us -> 128 us (0.934)
  Pallas kernels: 130 us -> 120 us
    pallas_call x1, Pallas kernels: 130 us -> 120 us  [body(): pl.pallas_call(run, out_shape=jax.ShapeDtypeStruct((tiers, height * cols,...]
where the time goes in v1:
time: 128 us; the launch traced here: 126 us
  Pallas kernels  120 us (94%)
  local copies, waits for them, and re-layouts  6.33 us (5%)
    pallas_call x1, Pallas kernels, body(): pl.pallas_call(run, out_shape=jax.ShapeDtypeStruct((tiers, height * cols,...  120 us
    unnamed x13, local copies, waits for them, and re-layouts  6.33 us

profile of v1, /device:TPU:19, one launch (start us, length us, event | category | flops | bytes accessed | tf_op | source)
XLA Modules:
  0.0 126.4 jit_solution(3494672492703712822)
XLA Ops:
  0.0 0.0 copy-start
  0.0 1.0 copy-done
  1.0 0.0 copy-start.1
  1.0 0.7 copy-done.1
  1.7 0.0 copy-start.2
  1.7 0.7 copy-done.2
  2.4 0.0 copy-start.3
  2.4 0.7 copy-done.3
  3.0 0.0 copy-start.4
  3.0 0.7 copy-done.4
  3.7 0.0 copy-start.5
  3.7 0.7 copy-done.5
  4.3 120.1 %shard_map.73 = f32[8,256,512]{2,1,0:T(8,128)S(1)} custom-call(f32[8,32,4096]{2,1,0:T(8,128)} %refs_0_.1, s32[32,4096]{1,0:T(8,128)S(1)} %copy-done, f32[64]{0:T(128)S(1)} %copy-done.1, s32[8]{0:T(128)S(1)} %copy-done.2, f32[4]{0:T(128)S(1)} %copy-done.3, f32[4]{0:T(128)S(1)} %copy-done.4, f32[4]{0:T(128)S(1)} %copy-done.5), custom_call_target="tpu_custom_call" | custom-call | tf_op jit(solution)/shard_map/pallas_call | solution.py:372
  124.4 2.0 %copy.9 = f32[8,256,512]{2,1,0:T(8,128)} copy(f32[8,256,512]{2,1,0:T(8,128)S(1)} %shard_map.73) | data formatting | bytes 8388608
Async XLA Ops:
  0.0 1.0 copy-start
  1.0 0.7 copy-start.1
  1.7 0.7 copy-start.2
  2.4 0.7 copy-start.3
  3.0 0.7 copy-start.4
  3.7 0.7 copy-start.5

commit v2 on v1

--- a/solution.py
+++ b/solution.py
@@ -15,11 +15,11 @@
     cols,
     heat,
     label,
-    flux_tab,
-    tier_lab,
-    lat_tab,
-    vert_tab,
-    share_tab,
+    flux_src,
+    tier_src,
+    lat_src,
+    vert_src,
+    share_src,
     out,
     ext,
     lab_ext,
@@ -33,6 +33,12 @@
     send_sem,
     recv_sem,
     own_sem,
+    flux_tab,
+    tier_lab,
+    lat_tab,
+    vert_tab,
+    share_tab,
+    small_sem,
 ):
     tiers, height, breadth = heat.shape
     tall = height + 2 * HALO
@@ -58,6 +64,21 @@
         label, lab_ext.at[pl.ds(HALO, height), pl.ds(LANES, breadth)], in_sem.at[1]
     )
     own_lab.start()
+
+    small = [
+        pltpu.make_async_copy(src, dst, small_sem.at[i])
+        for i, (src, dst) in enumerate(
+            (
+                (flux_src, flux_tab),
+                (tier_src, tier_lab),
+                (lat_src, lat_tab),
+                (vert_src, vert_tab),
+                (share_src, share_tab),
+            )
+        )
+    ]
+    for copy in small:
+        copy.start()
 
     barrier = pltpu.get_barrier_semaphore()
     for j in range(1, cols):
@@ -185,6 +206,8 @@
             look_up(at, first, HALO)
         return carry
 
+    for copy in small:
+        copy.wait()
     own_lab.wait()
     lax.fori_loop(0, breadth // piece, own_density, 0)
     own_heat.wait()
@@ -362,7 +385,6 @@
         tall = height + 2 * HALO
         width = breadth // cols
         wide = width + 2 * LANES
-        smem = pl.BlockSpec(memory_space=pltpu.SMEM)
         hbm = pl.BlockSpec(memory_space=pl.ANY)
         dma = pltpu.SemaphoreType.DMA
 
@@ -372,7 +394,7 @@
         return pl.pallas_call(
             run,
             out_shape=jax.ShapeDtypeStruct((tiers, height * cols, width), jnp.float32),
-            in_specs=[hbm, hbm, smem, smem, smem, smem, smem],
+            in_specs=[hbm] * 7,
             out_specs=hbm,
             scratch_shapes=[
                 pltpu.VMEM((tiers, tall, breadth + 2 * LANES), jnp.float32),
@@ -387,6 +409,11 @@
                 dma((cols,)),
                 dma((cols,)),
                 dma((1,)),
+                *[
+                    pltpu.SMEM(x.shape, x.dtype)
+                    for x in (flux_tab, tier_lab, lat_tab, vert_tab, share_tab)
+                ],
+                dma((5,)),
             ],
             compiler_params=pltpu.CompilerParams(
                 collective_id=0, has_side_effects=True, vmem_limit_bytes=48 * 2**20

time: 128 us -> 128 us (level)
  no operation moved by 1% of the time
where the time goes in v2:
time: 128 us; the launch traced here: 126 us
  Pallas kernels  120 us (94%)
  local copies, waits for them, and re-layouts  6.33 us (5%)
    pallas_call x1, Pallas kernels, body(): pl.pallas_call(run, out_shape=jax.ShapeDtypeStruct((tiers, height * cols,...  120 us
    unnamed x13, local copies, waits for them, and re-layouts  6.33 us

profile of v2, /device:TPU:19, one launch (start us, length us, event | category | flops | bytes accessed | tf_op | source)
XLA Modules:
  0.0 125.9 jit_solution(5288474819509850083)
XLA Ops:
  0.0 0.0 copy-start
  0.0 1.0 copy-done
  1.0 0.0 copy-start.1
  1.0 0.7 copy-done.1
  1.7 0.0 copy-start.2
  1.7 0.7 copy-done.2
  2.4 0.0 copy-start.3
  2.4 0.7 copy-done.3
  3.0 0.0 copy-start.4
  3.0 0.7 copy-done.4
  3.7 0.0 copy-start.5
  3.7 0.7 copy-done.5
  4.3 119.5 %shard_map.73 = f32[8,256,512]{2,1,0:T(8,128)S(1)} custom-call(f32[8,32,4096]{2,1,0:T(8,128)} %refs_0_.1, s32[32,4096]{1,0:T(8,128)S(1)} %copy-done, f32[64]{0:T(128)S(1)} %copy-done.1, s32[8]{0:T(128)S(1)} %copy-done.2, f32[4]{0:T(128)S(1)} %copy-done.3, f32[4]{0:T(128)S(1)} %copy-done.4, f32[4]{0:T(128)S(1)} %copy-done.5), custom_call_target="tpu_custom_call" | custom-call | tf_op jit(solution)/shard_map/pallas_call | solution.py:394
  123.9 2.0 %copy.9 = f32[8,256,512]{2,1,0:T(8,128)} copy(f32[8,256,512]{2,1,0:T(8,128)S(1)} %shard_map.73) | data formatting | bytes 8388608
Async XLA Ops:
  0.0 1.0 copy-start
  1.0 0.7 copy-start.1
  1.7 0.7 copy-start.2
  2.4 0.7 copy-start.3
  3.0 0.7 copy-start.4
  3.7 0.7 copy-start.5
